TPU v7x, 128 devices: a whole 4x4x4 slice. The times are simulated.
128 devices in a mesh: row: 8 (over y_lo, z), col: 16 (over x, y_hi, core).
Axes of the slice: x: 4, y: 4 (y_hi: 2, y_lo: 2; y = y_hi * 2 + y_lo), z: 4, core: 2. Of those that a mesh axis runs over, the one named last changes fastest.
Arguments:
- feats_one: bfloat16 [65536, 256], P(('row', 'col')), may hold values from -6 to 6
- feats_two: bfloat16 [65536, 256], P(('row', 'col')), may hold values from -6 to 6
- target_view: bfloat16 [65536, 256], P(('row', 'col')), may hold values from -6 to 6
- negatives: int32 [65536], P(('row', 'col')), may hold values from 0 to 511
- weight_one: bfloat16 [256, 256], replicated, may hold values from -0.375 to 0.375
- weight_two: bfloat16 [256, 256], replicated, may hold values from -0.375 to 0.375
- block_tiles: bfloat16 [81920, 128, 128], P(('row', 'col')), may hold values from -0.15625 to 0.15625
- tile_rows: int32 [81920], P(('row', 'col')), may hold values from 0 to 31
- tile_cols: int32 [81920], P(('row', 'col')), may hold values from 0 to 31
- block_counts: int32 [128], P(('row', 'col')), may hold values from 80 to 640, as said below
- need_rows: int32 [128, 16, 2], P(('row', 'col')), may hold values from 0 to 3, as said below
Outputs:
- grad_hidden: bfloat16 [65536, 256], P(('row', 'col'))
- grad_first: float32 [256, 256], replicated
- grad_second: float32 [256, 256], replicated
Inputs may be any that keep to these rules, and one draw needn't show every extreme that they name: `need_rows`: for each owner and source, the 2 entries are distinct. `block_counts`: live tiles of one block list.
All inputs are finite; a program needn't handle non-finite values.
Results may differ from a plain program's by a relative error of at most 0.0063.
Values may be sent and summed in bfloat16 or wider, within the bound.
No kernel may reach another device: no remote copies, remote signals or barrier semaphores. Data moves between devices by JAX's collectives and lax.ppermute only.
A program may use at most 192 MiB of HBM per device.

v0:
```python
import math
import jax
import jax.numpy as jnp
from jax import lax
from jax.sharding import PartitionSpec as P


def silu_slope(values):
    sig = jax.nn.sigmoid(values)
    return sig * (1.0 + values * (1.0 - sig))


def column_product(left, right):
    return lax.dot_general(
        left, right, (((0,), (0,)), ((), ())), preferred_element_type=jnp.float32
    )


def on_device(
    feats_one,
    feats_two,
    target_view,
    negatives,
    weight_one,
    weight_two,
    block_tiles,
    tile_rows,
    tile_cols,
    block_counts,
    need_rows,
):
    node_dev, features = feats_two.shape
    capacity, tile_size = (block_tiles.shape[0], block_tiles.shape[1])
    sources = lax.axis_size("col")
    row_group = lax.axis_size("row")
    tiles_dev = node_dev // tile_size
    slot_count = need_rows.shape[2]
    col_count = row_group * tiles_dev
    inverse_root = 1.0 / math.sqrt(features)
    weight_norm = 1.0 / math.sqrt(node_dev * row_group * sources)
    pre_two = jnp.dot(feats_two, weight_two, preferred_element_type=jnp.float32)
    hidden = jax.nn.silu(pre_two)
    partner_rows = hidden[negatives]
    target_full = target_view.astype(jnp.float32)
    s_pos = jnp.sum(hidden * target_full, axis=-1) * inverse_root
    s_neg = jnp.sum(hidden * partner_rows, axis=-1) * inverse_root
    prob_pos = jax.nn.sigmoid(-s_pos)
    prob_neg = jax.nn.sigmoid(s_neg)
    grad_out = -prob_pos[:, None] * target_full + prob_neg[:, None] * partner_rows
    grad_out = grad_out + jax.ops.segment_sum(
        prob_neg[:, None] * hidden, negatives, num_segments=node_dev
    )
    dpre_two = (grad_out * silu_slope(pre_two)).astype(jnp.bfloat16)
    grad_second = column_product(feats_two, dpre_two)
    grad_second = lax.psum(grad_second, ("row", "col"))
    message = lax.dot_general(
        dpre_two, weight_two, (((1,), (1,)), ((), ())), preferred_element_type=jnp.float32
    ).astype(jnp.bfloat16)
    gathered = lax.all_gather(message, "col", axis=0, tiled=True)
    buffer_tiles = gathered.reshape(sources * tiles_dev, tile_size, features)
    need_flat = need_rows[0].reshape(-1)
    slot_ids = jnp.arange(sources * slot_count, dtype=jnp.int32)
    local_tile = jnp.sum(
        jnp.where(tile_rows[:, None] == slot_ids[None, :], need_flat[None, :], 0), axis=1
    )
    row_tile = tile_rows // slot_count * tiles_dev + local_tile
    block_len = 128
    rounds = capacity // block_len
    live = (jnp.arange(capacity, dtype=jnp.int32) < block_counts[0]).astype(jnp.float32)
    column_ids = jnp.arange(col_count, dtype=jnp.int32)

    def add_block(summed_tiles, pieces):
        tile_part, row_part, col_part, live_part = pieces
        gathered_rows = buffer_tiles[row_part]
        contrib = jnp.einsum(
            "ktu,ktf->kuf", tile_part, gathered_rows, preferred_element_type=jnp.float32
        )
        selector = jnp.where(col_part[:, None] == column_ids[None, :], live_part[:, None], 0.0)
        placed = jnp.einsum(
            "kc,kuf->cuf",
            selector,
            contrib,
            precision=lax.Precision.HIGHEST,
            preferred_element_type=jnp.float32,
        )
        return (summed_tiles + placed, None)

    start_tiles = jnp.zeros((col_count, tile_size, features), jnp.float32)
    summed_tiles, _ = lax.scan(
        add_block,
        start_tiles,
        (
            block_tiles.reshape(rounds, block_len, tile_size, tile_size),
            row_tile.reshape(rounds, block_len),
            tile_cols.reshape(rounds, block_len),
            live.reshape(rounds, block_len),
        ),
    )
    column_total = lax.psum_scatter(
        summed_tiles.reshape(col_count * tile_size, features),
        "row",
        scatter_dimension=0,
        tiled=True,
    )
    grad_hidden = column_total.astype(jnp.bfloat16)
    pre_one = jnp.dot(feats_one, weight_one, preferred_element_type=jnp.float32)
    dpre_one = (grad_hidden.astype(jnp.float32) * silu_slope(pre_one)).astype(jnp.bfloat16)
    grad_first = column_product(feats_one, dpre_one)
    grad_first = lax.psum(grad_first, ("row", "col"))
    return (grad_hidden, grad_first * weight_norm, grad_second * weight_norm)


def solution(mesh):
    return jax.shard_map(
        on_device,
        mesh=mesh,
        in_specs=(
            P(("row", "col"), None),
            P(("row", "col"), None),
            P(("row", "col"), None),
            P(("row", "col")),
            P(),
            P(),
            P(("row", "col"), None, None),
            P(("row", "col")),
            P(("row", "col")),
            P(("row", "col")),
            P(("row", "col"), None, None),
        ),
        out_specs=(P(("row", "col"), None), P(), P()),
        check_vma=False,
    )
```

profile of v0, /device:TPU:1, one launch (start us, length us, event | category | flops | bytes accessed | tf_op | source)
XLA Modules:
  0.0 544.5 jit_solution(12721467284938459450)
XLA Ops:
  7.2 1.0 copy-done
  8.2 1.2 fusion.22
  9.5 0.2 copy.43
  9.7 0.7 compare_select_fusion.1
  10.4 1.6 gather_fusion.1
  11.9 0.2 copy.44
  12.5 0.2 broadcast_multiply_fusion
  12.6 0.2 copy.46
  12.8 0.2 copy.47
  13.1 3.5 scatter_fusion
  16.6 0.2 copy.48
  16.8 0.2 multiply_convert_fusion.1
  17.0 1.0 convolution_convert_fusion
  18.1 27.9 %copy.40 = bf16[640,128,128]{1,2,0:T(8,128)(2,1)} copy(bf16[640,128,128]{2,1,0:T(8,128)(2,1)} %param.19) | data formatting | bytes 41943040 | tf_op args[6]
  47.0 30.8 %all-gather.2.cloned.1.call-done = bf16[8192,256]{1,0:T(8,128)(2,1)} async-done(((bf16[512,256]{1,0:T(8,128)(2,1)}), bf16[8192,256]{1,0:T(8,128)(2,1)}) %all-gather.2.cloned.1.call-update) | async-done | bytes 4194320 | tf_op jit(solution)/shard_map/all_gather | solution.py:59
  77.8 241.0 %while.11 = (s32[]{:T(128)}, f32[32,128,256]{2,0,1:T(8,128)}, s32[5,128]{1,0:T(8,128)}, f32[5,128]{1,0:T(8,128)S(1)}, bf16[5,128,128,128]{2,3,1,0:T(8,128)(2,1)}...) while((s32[]{:T(128)}, f32[32,128,256]{2,0,1:T(8,128)}, ...), condition=%wide.region_5.6_spmd.clone, body=%wide.region_4.5_spmd.clone.sunk | while | flops 2686461440 | bytes 71313008 | solution.py:89
  77.8 8.7 %gather_fusion = bf16[128,128,256]{2,1,0:T(8,128)(2,1)} fusion(bf16[64,128,256]{2,1,0:T(8,128)(2,1)} %get-tuple-element.172, s32[1024]{0:T(1024)S(1)} %pad_clamp_fusion.3), kind=kCustom, calls=%fused_computation.clone.clone.1 | custom fusion | bytes 16777728 | tf_op jit(solution)/shard_map/while/body/eval_jaxpr/gather | solution.py:74
  86.5 12.8 %fusion.55 = f32[128,128,256]{2,1,0:T(8,128)} fusion(bf16[128,128,256]{2,1,0:T(8,128)(2,1)} %gather_fusion, bf16[5,128,128,128]{2,3,1,0:T(8,128)(2,1)} %get-tuple-element.170, s32[]{:T(128)} %get-tuple-element.157), kind=kOutput, calls=%fused_computation.6.clone.1 | convolution fusion | flops 1073741824 | bytes 29360640 | tf_op jit(solution)/shard_map/while/body/eval_jaxpr/ktu,ktf->kuf/dot_general | solution.py:75
  99.4 0.7 fusion.57
  100.0 25.4 %select_add_fusion.2 = f32[32,128,256]{2,0,1:T(8,128)} fusion(f32[32,128,256]{2,0,1:T(8,128)} %get-tuple-element.158, pred[]{:T(512)S(6)} %compare.5, f32[128,128,256]{2,1,0:T(8,128)} %fusion.55, f32[128]{0:T(128)S(1)} %fusion.56, s32[128]{0:T(128)S(1)} %fusion.57), kind=kOutput, calls=%fused_computation.8.clone.1 | convolution fusion | flops 1612718080 | bytes 25166848 | tf_op jit(solution)/shard_map/while/body/eval_jaxpr/kc,kuf->cuf/dot_general | solution.py:79
  125.5 8.7 %gather_fusion = bf16[128,128,256]{2,1,0:T(8,128)(2,1)} fusion(bf16[64,128,256]{2,1,0:T(8,128)(2,1)} %get-tuple-element.172, s32[1024]{0:T(1024)S(1)} %pad_clamp_fusion.3), kind=kCustom, calls=%fused_computation.clone.clone.1 | custom fusion | bytes 16777728 | tf_op jit(solution)/shard_map/while/body/eval_jaxpr/gather | solution.py:74
  134.2 12.8 %fusion.55 = f32[128,128,256]{2,1,0:T(8,128)} fusion(bf16[128,128,256]{2,1,0:T(8,128)(2,1)} %gather_fusion, bf16[5,128,128,128]{2,3,1,0:T(8,128)(2,1)} %get-tuple-element.170, s32[]{:T(128)} %get-tuple-element.157), kind=kOutput, calls=%fused_computation.6.clone.1 | convolution fusion | flops 1073741824 | bytes 29360640 | tf_op jit(solution)/shard_map/while/body/eval_jaxpr/ktu,ktf->kuf/dot_general | solution.py:75
  147.1 0.7 fusion.57
  147.8 26.0 %select_add_fusion.2 = f32[32,128,256]{2,0,1:T(8,128)} fusion(f32[32,128,256]{2,0,1:T(8,128)} %get-tuple-element.158, pred[]{:T(512)S(6)} %compare.5, f32[128,128,256]{2,1,0:T(8,128)} %fusion.55, f32[128]{0:T(128)S(1)} %fusion.56, s32[128]{0:T(128)S(1)} %fusion.57), kind=kOutput, calls=%fused_computation.8.clone.1 | convolution fusion | flops 1612718080 | bytes 25166848 | tf_op jit(solution)/shard_map/while/body/eval_jaxpr/kc,kuf->cuf/dot_general | solution.py:79
  173.8 8.7 %gather_fusion = bf16[128,128,256]{2,1,0:T(8,128)(2,1)} fusion(bf16[64,128,256]{2,1,0:T(8,128)(2,1)} %get-tuple-element.172, s32[1024]{0:T(1024)S(1)} %pad_clamp_fusion.3), kind=kCustom, calls=%fused_computation.clone.clone.1 | custom fusion | bytes 16777728 | tf_op jit(solution)/shard_map/while/body/eval_jaxpr/gather | solution.py:74
  182.6 12.8 %fusion.55 = f32[128,128,256]{2,1,0:T(8,128)} fusion(bf16[128,128,256]{2,1,0:T(8,128)(2,1)} %gather_fusion, bf16[5,128,128,128]{2,3,1,0:T(8,128)(2,1)} %get-tuple-element.170, s32[]{:T(128)} %get-tuple-element.157), kind=kOutput, calls=%fused_computation.6.clone.1 | convolution fusion | flops 1073741824 | bytes 29360640 | tf_op jit(solution)/shard_map/while/body/eval_jaxpr/ktu,ktf->kuf/dot_general | solution.py:75
  195.4 0.7 fusion.57
  196.1 26.0 %select_add_fusion.2 = f32[32,128,256]{2,0,1:T(8,128)} fusion(f32[32,128,256]{2,0,1:T(8,128)} %get-tuple-element.158, pred[]{:T(512)S(6)} %compare.5, f32[128,128,256]{2,1,0:T(8,128)} %fusion.55, f32[128]{0:T(128)S(1)} %fusion.56, s32[128]{0:T(128)S(1)} %fusion.57), kind=kOutput, calls=%fused_computation.8.clone.1 | convolution fusion | flops 1612718080 | bytes 25166848 | tf_op jit(solution)/shard_map/while/body/eval_jaxpr/kc,kuf->cuf/dot_general | solution.py:79
  222.2 8.8 %gather_fusion = bf16[128,128,256]{2,1,0:T(8,128)(2,1)} fusion(bf16[64,128,256]{2,1,0:T(8,128)(2,1)} %get-tuple-element.172, s32[1024]{0:T(1024)S(1)} %pad_clamp_fusion.3), kind=kCustom, calls=%fused_computation.clone.clone.1 | custom fusion | bytes 16777728 | tf_op jit(solution)/shard_map/while/body/eval_jaxpr/gather | solution.py:74
  230.9 12.8 %fusion.55 = f32[128,128,256]{2,1,0:T(8,128)} fusion(bf16[128,128,256]{2,1,0:T(8,128)(2,1)} %gather_fusion, bf16[5,128,128,128]{2,3,1,0:T(8,128)(2,1)} %get-tuple-element.170, s32[]{:T(128)} %get-tuple-element.157), kind=kOutput, calls=%fused_computation.6.clone.1 | convolution fusion | flops 1073741824 | bytes 29360640 | tf_op jit(solution)/shard_map/while/body/eval_jaxpr/ktu,ktf->kuf/dot_general | solution.py:75
  243.7 0.7 fusion.57
  244.4 26.0 %select_add_fusion.2 = f32[32,128,256]{2,0,1:T(8,128)} fusion(f32[32,128,256]{2,0,1:T(8,128)} %get-tuple-element.158, pred[]{:T(512)S(6)} %compare.5, f32[128,128,256]{2,1,0:T(8,128)} %fusion.55, f32[128]{0:T(128)S(1)} %fusion.56, s32[128]{0:T(128)S(1)} %fusion.57), kind=kOutput, calls=%fused_computation.8.clone.1 | convolution fusion | flops 1612718080 | bytes 25166848 | tf_op jit(solution)/shard_map/while/body/eval_jaxpr/kc,kuf->cuf/dot_general | solution.py:79
  270.5 8.7 %gather_fusion = bf16[128,128,256]{2,1,0:T(8,128)(2,1)} fusion(bf16[64,128,256]{2,1,0:T(8,128)(2,1)} %get-tuple-element.172, s32[1024]{0:T(1024)S(1)} %pad_clamp_fusion.3), kind=kCustom, calls=%fused_computation.clone.clone.1 | custom fusion | bytes 16777728 | tf_op jit(solution)/shard_map/while/body/eval_jaxpr/gather | solution.py:74
  279.2 12.8 %fusion.55 = f32[128,128,256]{2,1,0:T(8,128)} fusion(bf16[128,128,256]{2,1,0:T(8,128)(2,1)} %gather_fusion, bf16[5,128,128,128]{2,3,1,0:T(8,128)(2,1)} %get-tuple-element.170, s32[]{:T(128)} %get-tuple-element.157), kind=kOutput, calls=%fused_computation.6.clone.1 | convolution fusion | flops 1073741824 | bytes 29360640 | tf_op jit(solution)/shard_map/while/body/eval_jaxpr/ktu,ktf->kuf/dot_general | solution.py:75
  292.1 0.7 fusion.57
  292.8 26.0 %select_add_fusion.2 = f32[32,128,256]{2,0,1:T(8,128)} fusion(f32[32,128,256]{2,0,1:T(8,128)} %get-tuple-element.158, pred[]{:T(512)S(6)} %compare.5, f32[128,128,256]{2,1,0:T(8,128)} %fusion.55, f32[128]{0:T(128)S(1)} %fusion.56, s32[128]{0:T(128)S(1)} %fusion.57), kind=kOutput, calls=%fused_computation.8.clone.1 | convolution fusion | flops 1612718080 | bytes 25166848 | tf_op jit(solution)/shard_map/while/body/eval_jaxpr/kc,kuf->cuf/dot_general | solution.py:79
  318.8 5.9 %copy.49 = f32[32,128,256]{1,0,2:T(8,128)} copy(f32[32,128,256]{2,0,1:T(8,128)} %get-tuple-element.45) | data formatting | bytes 8388608 | tf_op jit(solution)/shard_map/while | solution.py:89
  324.8 8.0 %copy.62 = f32[32,8,32,128]{3,1,2,0:T(8,128)} copy(f32[32,8,32,128]{3,2,1,0:T(8,128)} %bitcast.62) | data formatting | bytes 8388608
  332.8 0.9 convolution_bitcast_fusion
  333.8 50.9 %reduce-scatter.2.cloned.1.call-done = f32[512,256]{0,1:T(8,128)} async-done(((f32[4096,256]{0,1:T(8,128)}), f32[512,256]{0,1:T(8,128)}) %reduce-scatter.2.cloned.1.call-update) | async-done | bytes 524304 | tf_op jit(solution)/shard_map/reduce_scatter | solution.py:99
  384.7 1.1 convert_element_type.26
  385.8 1.2 convolution_bitcast_fusion.1
  387.0 0.8 copy.52
  387.9 146.5 %all-reduce.3.cloned.1.call-done = (f32[256,256]{0,1:T(8,128)}, f32[256,256]{0,1:T(8,128)}) async-done(((f32[256,256]{0,1:T(8,128)}, f32[256,256]{0,1:T(8,128)}), (f32[256,256]{0,1:T(8,128)}, f32[256,256]{0,1:T(8,128)})) %all-reduce.3.cloned.1.call-update) | async-done | bytes 524304 | tf_op jit(solution)/shard_map/psum | solution.py:109
  534.4 1.0 broadcast_multiply_fusion.2
  535.3 0.8 copy.53
  536.2 1.0 broadcast_multiply_fusion.1
  537.1 0.8 copy.54
  (46 shorter events, 0.9 us)
Async XLA Ops:
  7.2 1.0 copy-start
  7.2 5.9 %copy-start.4 = (s32[512]{0:T(512)S(1)}, s32[512]{0:T(512)}, u32[]{:S(2)}) copy-start(s32[512]{0:T(512)} %param.16) | copy-start | bytes 6148
  7.2 4.9 copy-start.1
  7.2 70.6 %all-gather.2.cloned.1.call-start = ((), (), s32[]{:S(2)}) async-start(), calls=%async_computation.1 | async-start | bytes 4456448 | tf_op jit(solution)/shard_map/all_gather | solution.py:59
  12.3 4.7 copy-start.2
  18.0 366.7 %reduce-scatter.2.cloned.1.call-start = ((), (), s32[]{:S(2)}) async-start(), calls=%async_computation.2 | async-start | bytes 4718592 | tf_op jit(solution)/shard_map/reduce_scatter | solution.py:99
  18.1 27.9 %copy-start.5 = (s32[1,16,2]{1,2,0:T(2,128)S(1)}, s32[1,16,2]{1,2,0:T(2,128)}, u32[]{:S(2)}) copy-start(s32[1,16,2]{1,2,0:T(2,128)} %param.23) | copy-start | bytes 388
  18.1 28.8 %copy-start.3 = (s32[640]{0:T(1024)S(1)}, s32[640]{0:T(1024)}, u32[]{:S(2)}) copy-start(s32[640]{0:T(1024)} %param.20) | copy-start | bytes 7684
  324.8 61.0 %copy-start.6 = (bf16[512,256]{1,0:T(8,128)(2,1)S(1)}, bf16[512,256]{1,0:T(8,128)(2,1)}, u32[]{:S(2)}) copy-start(bf16[512,256]{1,0:T(8,128)(2,1)} %param.13) | copy-start | bytes 786436
  324.8 61.0 %copy-start.7 = (bf16[256,256]{1,0:T(8,128)(2,1)S(1)}, bf16[256,256]{1,0:T(8,128)(2,1)}, u32[]{:S(2)}) copy-start(bf16[256,256]{1,0:T(8,128)(2,1)} %param.17) | copy-start | bytes 393220
  332.8 201.6 %all-reduce.3.cloned.1.call-start = ((), (), s32[]{:S(2)}) async-start(), calls=%async_computation.3 | async-start | bytes 1048576 | tf_op jit(solution)/shard_map/psum | solution.py:109
Sparse Core Ops, SparseCore 0:
  18.2 59.5 all-gather.1
  332.9 51.7 reduce-scatter.1
  390.2 144.0 all-reduce.2
where the time goes:
time: 546 us; the launch traced here: 544 us
  waiting for transfers between devices  228 us (42%)
  matrix products  198 us (36%)
  local copies, waits for them, and re-layouts  95.4 us (17%)
  between operations  14.6 us (3%)
  other arithmetic  7.94 us (1%)
    psum x1, waiting for transfers between devices, on_device(): grad_first = lax.psum(grad_first, ('row', 'col'))  146 us
    dot_general x5, matrix products, add_block(): jnp.einsum('kc,kuf->cuf', selector, contrib, precision=lax.Precision.HIGH...  130 us
    dot_general x5, matrix products, add_block(): jnp.einsum('ktu,ktf->kuf', tile_part, gathered_rows, preferred_element_ty...  64.1 us
    reduce_scatter x1, waiting for transfers between devices, on_device(): lax.psum_scatter(summed_tiles.reshape(col_count * tile_size, features), '...  50.9 us
    gather x5, local copies, waits for them, and re-layouts, add_block(): gathered_rows = buffer_tiles[row_part]  43.7 us
    unnamed x23, local copies, waits for them, and re-layouts  39.7 us
    all_gather x1, waiting for transfers between devices, on_device(): gathered = lax.all_gather(message, 'col', axis=0, tiled=True)  30.8 us
  transfers between devices with their start and end apart: 3, of which 3 were waited for; matrix products, arithmetic and copies ran while one was open for 6% of the time, Pallas kernels for 0%

commit v1 on v0

--- a/solution.py
+++ b/solution.py
@@ -106,7 +106,7 @@
     pre_one = jnp.dot(feats_one, weight_one, preferred_element_type=jnp.float32)
     dpre_one = (grad_hidden.astype(jnp.float32) * silu_slope(pre_one)).astype(jnp.bfloat16)
     grad_first = column_product(feats_one, dpre_one)
-    grad_first = lax.psum(grad_first, ("row", "col"))
+    grad_first = lax.psum(lax.psum(grad_first, "col"), "row")
     return (grad_hidden, grad_first * weight_norm, grad_second * weight_norm)
 
 

time: 546 us -> 756 us (1.38)
  waiting for transfers between devices: 228 us -> 433 us
    psum x1 -> x3, waiting for transfers between devices: 146 us -> 350 us  [the longest x2 202 us: on_device(): grad_first = lax.psum(lax.psum(grad_first, 'col'), 'row')]
    unnamed x23 -> x27, local copies, waits for them, and re-layouts: 39.7 us -> 40.4 us
  transfers between devices with their start and end apart: 3 -> 5, of which waited for: 3 -> 5; matrix products, arithmetic and copies ran while one was open for 6% -> 4% of each run, Pallas kernels for 0% -> 0%
where the time goes in v1:
time: 756 us; the launch traced here: 750 us
  waiting for transfers between devices  433 us (57%)
  matrix products  198 us (26%)
  local copies, waits for them, and re-layouts  96.1 us (13%)
  between operations  14.7 us (2%)
  other arithmetic  7.94 us (1%)
    psum x2, waiting for transfers between devices, on_device(): grad_first = lax.psum(lax.psum(grad_first, 'col'), 'row')  202 us
    psum x1, waiting for transfers between devices, on_device(): grad_second = lax.psum(grad_second, ('row', 'col'))  149 us
    dot_general x5, matrix products, add_block(): jnp.einsum('kc,kuf->cuf', selector, contrib, precision=lax.Precision.HIGH...  130 us
    dot_general x5, matrix products, add_block(): jnp.einsum('ktu,ktf->kuf', tile_part, gathered_rows, preferred_element_ty...  64.1 us
    reduce_scatter x1, waiting for transfers between devices, on_device(): lax.psum_scatter(summed_tiles.reshape(col_count * tile_size, features), '...  51.9 us
    gather x5, local copies, waits for them, and re-layouts, add_block(): gathered_rows = buffer_tiles[row_part]  43.7 us
    unnamed x27, local copies, waits for them, and re-layouts  40.4 us
    all_gather x1, waiting for transfers between devices, on_device(): gathered = lax.all_gather(message, 'col', axis=0, tiled=True)  30.8 us
  transfers between devices with their start and end apart: 5, of which 5 were waited for; matrix products, arithmetic and copies ran while one was open for 4% of the time, Pallas kernels for 0%

profile of v1, /device:TPU:1, one launch (start us, length us, event | category | flops | bytes accessed | tf_op | source)
XLA Modules:
  0.0 750.3 jit_solution(14213239009526577246)
XLA Ops:
  7.2 1.0 copy-done
  8.2 1.2 fusion.22
  9.7 0.7 compare_select_fusion.1
  10.4 1.6 gather_fusion.1
  11.9 0.2 copy.44
  12.6 0.2 copy.46
  13.1 3.5 scatter_fusion
  16.6 0.2 copy.48
  16.8 0.2 multiply_convert_fusion.1
  17.0 0.7 copy-done.1
  17.7 1.0 convolution_convert_fusion
  18.8 27.9 %copy.40 = bf16[640,128,128]{1,2,0:T(8,128)(2,1)} copy(bf16[640,128,128]{2,1,0:T(8,128)(2,1)} %param.19) | data formatting | bytes 41943040 | tf_op args[6]
  47.7 30.8 %all-gather.2.cloned.1.call-done = bf16[8192,256]{1,0:T(8,128)(2,1)} async-done(((bf16[512,256]{1,0:T(8,128)(2,1)}), bf16[8192,256]{1,0:T(8,128)(2,1)}) %all-gather.2.cloned.1.call-update) | async-done | bytes 4194320 | tf_op jit(solution)/shard_map/all_gather | solution.py:59
  78.5 241.0 %while.11 = (s32[]{:T(128)}, f32[32,128,256]{2,0,1:T(8,128)}, s32[5,128]{1,0:T(8,128)}, f32[5,128]{1,0:T(8,128)S(1)}, bf16[5,128,128,128]{2,3,1,0:T(8,128)(2,1)}...) while((s32[]{:T(128)}, f32[32,128,256]{2,0,1:T(8,128)}, ...), condition=%wide.region_5.6_spmd.clone, body=%wide.region_4.5_spmd.clone.sunk | while | flops 2686461440 | bytes 71313008 | solution.py:89
  78.5 8.7 %gather_fusion = bf16[128,128,256]{2,1,0:T(8,128)(2,1)} fusion(bf16[64,128,256]{2,1,0:T(8,128)(2,1)} %get-tuple-element.170, s32[1024]{0:T(1024)S(1)} %pad_clamp_fusion.3), kind=kCustom, calls=%fused_computation.clone.clone.1 | custom fusion | bytes 16777728 | tf_op jit(solution)/shard_map/while/body/eval_jaxpr/gather | solution.py:74
  87.2 12.8 %fusion.55 = f32[128,128,256]{2,1,0:T(8,128)} fusion(bf16[128,128,256]{2,1,0:T(8,128)(2,1)} %gather_fusion, bf16[5,128,128,128]{2,3,1,0:T(8,128)(2,1)} %get-tuple-element.168, s32[]{:T(128)} %get-tuple-element.155), kind=kOutput, calls=%fused_computation.6.clone.1 | convolution fusion | flops 1073741824 | bytes 29360640 | tf_op jit(solution)/shard_map/while/body/eval_jaxpr/ktu,ktf->kuf/dot_general | solution.py:75
  100.1 0.7 fusion.57
  100.7 25.4 %select_add_fusion.2 = f32[32,128,256]{2,0,1:T(8,128)} fusion(f32[32,128,256]{2,0,1:T(8,128)} %get-tuple-element.156, pred[]{:T(512)S(6)} %compare.5, f32[128,128,256]{2,1,0:T(8,128)} %fusion.55, f32[128]{0:T(128)S(1)} %fusion.56, s32[128]{0:T(128)S(1)} %fusion.57), kind=kOutput, calls=%fused_computation.8.clone.1 | convolution fusion | flops 1612718080 | bytes 25166848 | tf_op jit(solution)/shard_map/while/body/eval_jaxpr/kc,kuf->cuf/dot_general | solution.py:79
  126.2 8.7 %gather_fusion = bf16[128,128,256]{2,1,0:T(8,128)(2,1)} fusion(bf16[64,128,256]{2,1,0:T(8,128)(2,1)} %get-tuple-element.170, s32[1024]{0:T(1024)S(1)} %pad_clamp_fusion.3), kind=kCustom, calls=%fused_computation.clone.clone.1 | custom fusion | bytes 16777728 | tf_op jit(solution)/shard_map/while/body/eval_jaxpr/gather | solution.py:74
  134.9 12.8 %fusion.55 = f32[128,128,256]{2,1,0:T(8,128)} fusion(bf16[128,128,256]{2,1,0:T(8,128)(2,1)} %gather_fusion, bf16[5,128,128,128]{2,3,1,0:T(8,128)(2,1)} %get-tuple-element.168, s32[]{:T(128)} %get-tuple-element.155), kind=kOutput, calls=%fused_computation.6.clone.1 | convolution fusion | flops 1073741824 | bytes 29360640 | tf_op jit(solution)/shard_map/while/body/eval_jaxpr/ktu,ktf->kuf/dot_general | solution.py:75
  147.8 0.7 fusion.57
  148.5 26.0 %select_add_fusion.2 = f32[32,128,256]{2,0,1:T(8,128)} fusion(f32[32,128,256]{2,0,1:T(8,128)} %get-tuple-element.156, pred[]{:T(512)S(6)} %compare.5, f32[128,128,256]{2,1,0:T(8,128)} %fusion.55, f32[128]{0:T(128)S(1)} %fusion.56, s32[128]{0:T(128)S(1)} %fusion.57), kind=kOutput, calls=%fused_computation.8.clone.1 | convolution fusion | flops 1612718080 | bytes 25166848 | tf_op jit(solution)/shard_map/while/body/eval_jaxpr/kc,kuf->cuf/dot_general | solution.py:79
  174.5 8.7 %gather_fusion = bf16[128,128,256]{2,1,0:T(8,128)(2,1)} fusion(bf16[64,128,256]{2,1,0:T(8,128)(2,1)} %get-tuple-element.170, s32[1024]{0:T(1024)S(1)} %pad_clamp_fusion.3), kind=kCustom, calls=%fused_computation.clone.clone.1 | custom fusion | bytes 16777728 | tf_op jit(solution)/shard_map/while/body/eval_jaxpr/gather | solution.py:74
  183.3 12.8 %fusion.55 = f32[128,128,256]{2,1,0:T(8,128)} fusion(bf16[128,128,256]{2,1,0:T(8,128)(2,1)} %gather_fusion, bf16[5,128,128,128]{2,3,1,0:T(8,128)(2,1)} %get-tuple-element.168, s32[]{:T(128)} %get-tuple-element.155), kind=kOutput, calls=%fused_computation.6.clone.1 | convolution fusion | flops 1073741824 | bytes 29360640 | tf_op jit(solution)/shard_map/while/body/eval_jaxpr/ktu,ktf->kuf/dot_general | solution.py:75
  196.1 0.7 fusion.57
  196.8 26.0 %select_add_fusion.2 = f32[32,128,256]{2,0,1:T(8,128)} fusion(f32[32,128,256]{2,0,1:T(8,128)} %get-tuple-element.156, pred[]{:T(512)S(6)} %compare.5, f32[128,128,256]{2,1,0:T(8,128)} %fusion.55, f32[128]{0:T(128)S(1)} %fusion.56, s32[128]{0:T(128)S(1)} %fusion.57), kind=kOutput, calls=%fused_computation.8.clone.1 | convolution fusion | flops 1612718080 | bytes 25166848 | tf_op jit(solution)/shard_map/while/body/eval_jaxpr/kc,kuf->cuf/dot_general | solution.py:79
  222.9 8.8 %gather_fusion = bf16[128,128,256]{2,1,0:T(8,128)(2,1)} fusion(bf16[64,128,256]{2,1,0:T(8,128)(2,1)} %get-tuple-element.170, s32[1024]{0:T(1024)S(1)} %pad_clamp_fusion.3), kind=kCustom, calls=%fused_computation.clone.clone.1 | custom fusion | bytes 16777728 | tf_op jit(solution)/shard_map/while/body/eval_jaxpr/gather | solution.py:74
  231.6 12.8 %fusion.55 = f32[128,128,256]{2,1,0:T(8,128)} fusion(bf16[128,128,256]{2,1,0:T(8,128)(2,1)} %gather_fusion, bf16[5,128,128,128]{2,3,1,0:T(8,128)(2,1)} %get-tuple-element.168, s32[]{:T(128)} %get-tuple-element.155), kind=kOutput, calls=%fused_computation.6.clone.1 | convolution fusion | flops 1073741824 | bytes 29360640 | tf_op jit(solution)/shard_map/while/body/eval_jaxpr/ktu,ktf->kuf/dot_general | solution.py:75
  244.4 0.7 fusion.57
  245.1 26.0 %select_add_fusion.2 = f32[32,128,256]{2,0,1:T(8,128)} fusion(f32[32,128,256]{2,0,1:T(8,128)} %get-tuple-element.156, pred[]{:T(512)S(6)} %compare.5, f32[128,128,256]{2,1,0:T(8,128)} %fusion.55, f32[128]{0:T(128)S(1)} %fusion.56, s32[128]{0:T(128)S(1)} %fusion.57), kind=kOutput, calls=%fused_computation.8.clone.1 | convolution fusion | flops 1612718080 | bytes 25166848 | tf_op jit(solution)/shard_map/while/body/eval_jaxpr/kc,kuf->cuf/dot_general | solution.py:79
  271.2 8.7 %gather_fusion = bf16[128,128,256]{2,1,0:T(8,128)(2,1)} fusion(bf16[64,128,256]{2,1,0:T(8,128)(2,1)} %get-tuple-element.170, s32[1024]{0:T(1024)S(1)} %pad_clamp_fusion.3), kind=kCustom, calls=%fused_computation.clone.clone.1 | custom fusion | bytes 16777728 | tf_op jit(solution)/shard_map/while/body/eval_jaxpr/gather | solution.py:74
  279.9 12.8 %fusion.55 = f32[128,128,256]{2,1,0:T(8,128)} fusion(bf16[128,128,256]{2,1,0:T(8,128)(2,1)} %gather_fusion, bf16[5,128,128,128]{2,3,1,0:T(8,128)(2,1)} %get-tuple-element.168, s32[]{:T(128)} %get-tuple-element.155), kind=kOutput, calls=%fused_computation.6.clone.1 | convolution fusion | flops 1073741824 | bytes 29360640 | tf_op jit(solution)/shard_map/while/body/eval_jaxpr/ktu,ktf->kuf/dot_general | solution.py:75
  292.8 0.7 fusion.57
  293.5 26.0 %select_add_fusion.2 = f32[32,128,256]{2,0,1:T(8,128)} fusion(f32[32,128,256]{2,0,1:T(8,128)} %get-tuple-element.156, pred[]{:T(512)S(6)} %compare.5, f32[128,128,256]{2,1,0:T(8,128)} %fusion.55, f32[128]{0:T(128)S(1)} %fusion.56, s32[128]{0:T(128)S(1)} %fusion.57), kind=kOutput, calls=%fused_computation.8.clone.1 | convolution fusion | flops 1612718080 | bytes 25166848 | tf_op jit(solution)/shard_map/while/body/eval_jaxpr/kc,kuf->cuf/dot_general | solution.py:79
  319.5 5.9 copy.49
  325.5 8.0 %copy.62 = f32[32,8,32,128]{3,1,2,0:T(8,128)} copy(f32[32,8,32,128]{3,2,1,0:T(8,128)} %bitcast.62) | data formatting | bytes 8388608
  333.6 51.9 %reduce-scatter.2.cloned.1.call-done = f32[512,256]{0,1:T(8,128)} async-done(((f32[4096,256]{0,1:T(8,128)}), f32[512,256]{0,1:T(8,128)}) %reduce-scatter.2.cloned.1.call-update) | async-done | bytes 524304 | tf_op jit(solution)/shard_map/reduce_scatter | solution.py:99
  385.4 1.1 convert_element_type.26
  386.5 1.2 convolution_bitcast_fusion.1
  387.8 0.9 convolution_bitcast_fusion
  388.8 135.5 %all-reduce.4.cloned.1.call-done = f32[256,256]{0,1:T(8,128)} async-done(((f32[256,256]{0,1:T(8,128)}), f32[256,256]{0,1:T(8,128)}) %all-reduce.4.cloned.1.call-update) | async-done | bytes 262160 | tf_op jit(solution)/shard_map/psum | solution.py:109
  524.3 148.6 %all-reduce.8.cloned.1.call-done = f32[256,256]{0,1:T(8,128)} async-done(((f32[256,256]{0,1:T(8,128)}), f32[256,256]{0,1:T(8,128)}) %all-reduce.8.cloned.1.call-update) | async-done | bytes 262160 | tf_op jit(solution)/shard_map/psum | solution.py:55
  672.9 1.0 broadcast_multiply_fusion.1
  673.9 0.8 copy.54
  674.7 0.8 copy.52
  675.6 66.4 %all-reduce.6.cloned.1.call-done = f32[256,256]{0,1:T(8,128)} async-done(((f32[256,256]{0,1:T(8,128)}), f32[256,256]{0,1:T(8,128)}) %all-reduce.6.cloned.1.call-update) | async-done | bytes 262160 | tf_op jit(solution)/shard_map/psum | solution.py:109
  742.0 1.0 broadcast_multiply_fusion.2
  742.9 0.8 copy.53
  (56 shorter events, 1.6 us)
Async XLA Ops:
  7.2 1.0 copy-start
  7.2 5.9 copy-start.6
  7.2 4.9 copy-start.3
  7.2 71.3 %all-gather.2.cloned.1.call-start = ((), (), s32[]{:S(2)}) async-start(), calls=%async_computation.1 | async-start | bytes 4456448 | tf_op jit(solution)/shard_map/all_gather | solution.py:59
  12.3 5.4 copy-start.4
  17.0 0.7 copy-start.1
  18.7 366.7 %reduce-scatter.2.cloned.1.call-start = ((), (), s32[]{:S(2)}) async-start(), calls=%async_computation.2 | async-start | bytes 4718592 | tf_op jit(solution)/shard_map/reduce_scatter | solution.py:99
  18.8 27.9 %copy-start.7 = (s32[1,16,2]{1,2,0:T(2,128)S(1)}, s32[1,16,2]{1,2,0:T(2,128)}, u32[]{:S(2)}) copy-start(s32[1,16,2]{1,2,0:T(2,128)} %param.23) | copy-start | bytes 388
  18.8 28.8 %copy-start.5 = (s32[640]{0:T(1024)S(1)}, s32[640]{0:T(1024)}, u32[]{:S(2)}) copy-start(s32[640]{0:T(1024)} %param.20) | copy-start | bytes 7684
  325.5 61.1 %copy-start.8 = (bf16[512,256]{1,0:T(8,128)(2,1)S(1)}, bf16[512,256]{1,0:T(8,128)(2,1)}, u32[]{:S(2)}) copy-start(bf16[512,256]{1,0:T(8,128)(2,1)} %param.13) | copy-start | bytes 786436
  325.5 61.1 %copy-start.9 = (bf16[256,256]{1,0:T(8,128)(2,1)S(1)}, bf16[256,256]{1,0:T(8,128)(2,1)}, u32[]{:S(2)}) copy-start(bf16[256,256]{1,0:T(8,128)(2,1)} %param.17) | copy-start | bytes 393220
  325.5 62.4 %copy-start.2 = (bf16[512,256]{0,1:T(8,128)(2,1)S(1)}, bf16[512,256]{0,1:T(8,128)(2,1)}, u32[]{:S(2)}) copy-start(bf16[512,256]{0,1:T(8,128)(2,1)} %copy-done.1) | copy-start | bytes 786436
  333.5 190.8 %all-reduce.4.cloned.1.call-start = ((), (), s32[]{:S(2)}) async-start(), calls=%async_computation.3 | async-start | bytes 524288 | tf_op jit(solution)/shard_map/psum | solution.py:109
  387.8 285.2 %all-reduce.8.cloned.1.call-start = ((), (), s32[]{:S(2)}) async-start(), calls=%async_computation.5 | async-start | bytes 524288 | tf_op jit(solution)/shard_map/psum | solution.py:55
  388.8 353.2 %all-reduce.6.cloned.1.call-start = ((), (), s32[]{:S(2)}) async-start(), calls=%async_computation.4 | async-start | bytes 524288 | tf_op jit(solution)/shard_map/psum | solution.py:109
Sparse Core Ops, SparseCore 0:
  18.8 59.5 all-gather.1
  333.6 51.7 reduce-scatter.1
  388.5 135.7 all-reduce.3
  530.2 142.6 all-reduce.7
  675.4 66.5 all-reduce.5
